TPU v7x, 32 devices: a whole 2x2x4 slice. The times are simulated.
32 devices in a mesh: ctx: 16 (over z, x, core), tp: 2 (over y).
Axes of the slice: x: 2, y: 2, z: 4, core: 2. Of those that a mesh axis runs over, the one named last changes fastest.
Arguments:
- doc_lengths: int32 [32], replicated, may hold values from 1 to 512, 2048 in all
- ssm_x: bfloat16 [2048, 8192], P('ctx', 'tp'), may hold values from -6 to 6
- ssm_gate: bfloat16 [2048, 8192], P('ctx', 'tp'), may hold values from -6 to 6
- ssm_b: bfloat16 [2048, 2048], P('ctx', 'tp'), may hold values from -6 to 6
- ssm_c: bfloat16 [2048, 2048], P('ctx', 'tp'), may hold values from -0.375 to 0.375
- step_size: float32 [2048, 128], P('ctx', 'tp'), as said below
- decay_rate: float32 [128], P('tp'), as said below
- norm_weight: float32 [8192], P('tp'), may hold values from 0.1 to 1.9
- queries: bfloat16 [2048, 8192], P('ctx', 'tp'), may hold values from -96 to 96
- keys: bfloat16 [2048, 1024], P('ctx', 'tp'), may hold values from -4 to 4
- values: bfloat16 [2048, 1024], P('ctx', 'tp'), may hold values from -6 to 6
Outputs:
- mixed: bfloat16 [2048, 8192], P(('ctx', 'tp'))
- attended: bfloat16 [2048, 8192], P(('ctx', 'tp'))
Inputs may be any that keep to these rules, and one draw needn't show every extreme that they name: `doc_lengths`: every document has at least one token; the longest has exactly 512. `step_size`: Positive. `decay_rate`: Positive, at most 0.04.
All inputs are finite; a program needn't handle non-finite values.
Results may differ from a plain program's by a relative error of at most 0.0049.
Values may be sent and summed in bfloat16 or wider, within the bound.
A program may use at most 192 MiB of HBM per device.

v0:
```python
import jax
import jax.numpy as jnp
from jax import lax
from jax.sharding import PartitionSpec as P

HEADS = 128
GROUPS = 8
ATT_DIM = 128
DOC_DEVS = 4
NEG_LARGE = -1e30


def for_sending(x):
    return jax.tree.map(lambda a: a.astype(jnp.bfloat16) if a.dtype == jnp.float32 else a, x)


def passed_along(block, axis, distance):
    devices = range(lax.axis_size(axis))
    route = [(i - distance, i) for i in devices if i - distance in devices]
    return lax.ppermute(block, axis, route)


def doc_starts(doc_lengths):
    return jnp.cumsum(doc_lengths) - doc_lengths


def doc_index(positions, starts):
    return jnp.sum((starts[None, :] <= positions[:, None]).astype(jnp.int32), axis=1) - 1


def block_terms(ssm_x, ssm_b, ssm_c, step_size, decay_rate, doc_ids, prev_id, group_heads):
    tok_rows = ssm_x.shape[0]
    head_count = step_size.shape[1]
    group_count = head_count // group_heads
    head_size = ssm_x.shape[1] // head_count
    state_size = ssm_b.shape[1] // group_count
    inputs = ssm_x.reshape(tok_rows, group_count, group_heads, head_size)
    in_proj = ssm_b.reshape(tok_rows, group_count, state_size)
    out_proj = ssm_c.reshape(tok_rows, group_count, state_size)
    log_decay = -(step_size * decay_rate[None, :])
    cumulative = jnp.cumsum(log_decay, axis=0)
    same_doc = doc_ids[:, None] == doc_ids[None, :]
    causal = jnp.arange(tok_rows)[:, None] >= jnp.arange(tok_rows)[None, :]
    allowed = (same_doc & causal)[None]
    spread = cumulative.T[:, :, None] - cumulative.T[:, None, :]
    weights = (
        jnp.where(allowed, jnp.exp(jnp.where(allowed, spread, 0.0)), 0.0) * step_size.T[:, None, :]
    )
    intersection = jnp.einsum("tgn,sgn->gts", out_proj, in_proj, preferred_element_type=jnp.float32)
    mixing = (
        weights.reshape(group_count, group_heads, tok_rows, tok_rows) * intersection[:, None]
    ).astype(jnp.bfloat16)
    y_intra = jnp.einsum("ghts,sghp->tghp", mixing, inputs, preferred_element_type=jnp.float32)
    final_sum = cumulative[-1]
    tail = (
        jnp.exp(final_sum[None, :] - cumulative)
        * step_size
        * (doc_ids == doc_ids[-1]).astype(jnp.float32)[:, None]
    )
    scaled = (
        inputs.astype(jnp.float32) * tail.reshape(tok_rows, group_count, group_heads)[..., None]
    ).astype(jnp.bfloat16)
    state_local = jnp.einsum("sghp,sgn->ghpn", scaled, in_proj, preferred_element_type=jnp.float32)
    entry = jnp.exp(cumulative) * (doc_ids == prev_id).astype(jnp.float32)[:, None]
    transmit = jnp.exp(final_sum) * (doc_ids[-1] == prev_id).astype(jnp.float32)
    return (y_intra, state_local, entry, transmit.reshape(group_count, group_heads))


def finish_rows(y_intra, entry, carried, ssm_c, ssm_gate, norm_weight):
    tok_rows, group_count, group_heads, head_size = y_intra.shape
    out_proj = ssm_c.reshape(tok_rows, group_count, -1).astype(jnp.float32)
    incoming = jnp.einsum("tgn,ghpn->tghp", out_proj, carried, precision=lax.Precision.HIGHEST)
    mixer_out = y_intra + incoming * entry.reshape(tok_rows, group_count, group_heads)[..., None]
    gate_vals = ssm_gate.reshape(tok_rows, group_count, group_heads, head_size).astype(jnp.float32)
    gated = (mixer_out * jax.nn.silu(gate_vals)).reshape(
        tok_rows, group_count, group_heads * head_size
    )
    factor = lax.rsqrt(jnp.mean(gated * gated, axis=2, keepdims=True) + 1e-05)
    return ((gated * factor).reshape(tok_rows, -1) * norm_weight[None, :]).astype(jnp.bfloat16)


def chain_states(earlier, later):
    return (earlier[0] * later[0], later[0][:, :, None, None] * earlier[1] + later[1])


def attention_update(
    carry, query_rows, key_block, value_block, key_pos, query_pos, query_doc, starts
):
    running_max, running_sum, running_acc = carry
    block_rows = key_block.shape[0]
    kv_local = key_block.shape[1] // ATT_DIM
    key_heads = key_block.reshape(block_rows, kv_local, ATT_DIM)
    value_heads = value_block.reshape(block_rows, kv_local, ATT_DIM)
    key_doc = doc_index(key_pos, starts)
    allowed = (query_doc[:, None] == key_doc[None, :]) & (key_pos[None, :] <= query_pos[:, None])
    scores = jnp.einsum(
        "tngd,knd->ngtk", query_rows, key_heads, preferred_element_type=jnp.float32
    ) * ATT_DIM ** (-0.5)
    scores = jnp.where(allowed[None, None], scores, -jnp.inf)
    new_max = jnp.maximum(running_max, jnp.max(scores, axis=3))
    probs = jnp.exp(scores - new_max[..., None])
    factor = jnp.exp(running_max - new_max)
    new_sum = running_sum * factor + jnp.sum(probs, axis=3)
    weighted = jnp.einsum(
        "ngtk,knd->ngtd",
        probs.astype(jnp.bfloat16),
        value_heads,
        preferred_element_type=jnp.float32,
    )
    return (new_max, new_sum, running_acc * factor[..., None] + weighted)


def local(
    doc_lengths,
    ssm_x,
    ssm_gate,
    ssm_b,
    ssm_c,
    step_size,
    decay_rate,
    norm_weight,
    queries,
    keys,
    values,
):
    tok_rows = ssm_x.shape[0]
    ctx_index = lax.axis_index("ctx")
    begin = ctx_index * tok_rows
    positions = begin + jnp.arange(tok_rows, dtype=jnp.int32)
    starts = doc_starts(doc_lengths)
    doc_ids = doc_index(positions, starts)
    prev_id = doc_index(jnp.reshape(begin - 1, (1,)), starts)[0]
    group_heads = HEADS // GROUPS
    y_intra, state_local, entry, transmit = block_terms(
        ssm_x, ssm_b, ssm_c, step_size, decay_rate, doc_ids, prev_id, group_heads
    )
    merged = (transmit, state_local)
    for level_bit in range(DOC_DEVS.bit_length() - 1):
        earlier = passed_along(
            (for_sending(merged[0]), for_sending(merged[1])), "ctx", 1 << level_bit
        )
        merged = chain_states(earlier, merged)
    carried = passed_along(merged[1], "ctx", 1)
    mixed_rows = finish_rows(y_intra, entry, carried, ssm_c, ssm_gate, norm_weight)
    kv_local = keys.shape[1] // ATT_DIM
    q_groups = queries.shape[1] // (kv_local * ATT_DIM)
    query_rows = queries.reshape(tok_rows, kv_local, q_groups, ATT_DIM)
    floor_start = jnp.max(jnp.where(starts <= begin, starts, 0))
    query_last = begin + tok_rows - 1
    carry_shape = (kv_local, q_groups, tok_rows)
    initial = (
        jnp.full(carry_shape, NEG_LARGE, jnp.float32),
        jnp.zeros(carry_shape, jnp.float32),
        jnp.zeros(carry_shape + (ATT_DIM,), jnp.float32),
    )

    def visit(carry, key_block, value_block, key_begin):
        block_rows = key_block.shape[0]
        needed = (key_begin <= query_last) & (key_begin + block_rows - 1 >= floor_start)

        def update(inner):
            key_pos = key_begin + jnp.arange(block_rows, dtype=jnp.int32)
            return attention_update(
                inner, query_rows, key_block, value_block, key_pos, positions, doc_ids, starts
            )

        def unchanged(inner):
            return inner

        return lax.cond(needed, update, unchanged, carry)

    totals = visit(initial, keys, values, begin)
    for hop_count in range(1, DOC_DEVS + 1):
        near_keys, near_values = passed_along((keys, values), "ctx", hop_count)
        totals = visit(totals, near_keys, near_values, begin - hop_count * tok_rows)
    final_out = totals[2] / totals[1][..., None]
    attended_rows = (
        jnp.transpose(final_out, (2, 0, 1, 3)).reshape(tok_rows, -1).astype(jnp.bfloat16)
    )
    mixed_local, attended_local = (
        lax.all_to_all(mixed_rows, "tp", split_axis=0, concat_axis=1, tiled=True),
        lax.all_to_all(attended_rows, "tp", split_axis=0, concat_axis=1, tiled=True),
    )
    return (mixed_local, attended_local)


def solution(mesh):
    return jax.shard_map(
        local,
        mesh=mesh,
        in_specs=(
            P(),
            P("ctx", "tp"),
            P("ctx", "tp"),
            P("ctx", "tp"),
            P("ctx", "tp"),
            P("ctx", "tp"),
            P("tp"),
            P("tp"),
            P("ctx", "tp"),
            P("ctx", "tp"),
            P("ctx", "tp"),
        ),
        out_specs=(P(("ctx", "tp"), None), P(("ctx", "tp"), None)),
        check_vma=False,
    )
```

profile of v0, /device:TPU:26, one launch (start us, length us, event | category | flops | bytes accessed | tf_op | source)
XLA Modules:
  0.0 229.4 jit_solution(9776765901697887157)
XLA Ops:
  0.7 0.8 copy.164
  1.6 1.3 fusion.53
  5.7 0.8 copy.170
  6.6 0.8 multiply_negate_fusion
  8.4 1.6 copy.169
  10.2 3.4 %fusion.61 = (bf16[4,16,64,256]{3,2,1,0:T(8,128)(2,1)}, f32[4,16,64,256]{3,2,1,0:T(8,128)}) fusion(bf16[128,4,256,1]{2,1,0,3:T(4,128)(2,1)S(1)} %bitcast.87, bf16[128,4,16,64]{0,3,2,1:T(8,128)(2,1)S(1)} %bitcast.80, f32[128,4,16]{0,2,1:T(8,128)S(1)} %bitcast.100), kind=kOutput, calls=%fused_computation.124 | convolution fusion | flops 271056896 | bytes 7634944 | tf_op jit(solution)/shard_map/sghp,sgn->ghpn/dot_general | solution.py:63
  13.6 1.9 collective-permute-start.1
  16.2 24.9 %collective-permute-done.1 = bf16[4,16,64,256]{3,2,1,0:T(8,128)(2,1)S(1)} collective-permute-done((bf16[4,16,64,256]{3,2,1,0:T(8,128)(2,1)}, bf16[4,16,64,256]{3,2,1,0:T(8,128)(2,1)S(1)}, u32[]{:S(2)}, u32[]{:S(2)}) %collective-permute-start.1) | collective-permute-done | bytes 2097184 | tf_op jit(solution)/shard_map/ppermute | solution.py:20
  41.1 2.9 %fusion.31 = bf16[4,16,64,256]{3,2,1,0:T(8,128)(2,1)S(1)} fusion(f32[4,16,64,256]{3,2,1,0:T(8,128)} %get-tuple-element.411, bf16[4,16,64,256]{3,2,1,0:T(8,128)(2,1)S(1)} %collective-permute-done.1, f32[4,16]{1,0:T(4,128)S(1)} %mul.225), kind=kLoop, calls=%fused_computation.74 | loop fusion | flops 4194304 | bytes 8388864 | tf_op jit(solution)/shard_map/convert_element_type | solution.py:14
  44.0 1.3 collective-permute-start.2
  45.3 1.9 collective-permute-start
  47.2 41.3 %collective-permute-done = bf16[4,16]{1,0:T(4,128)(2,1)S(1)} collective-permute-done((bf16[4,16]{1,0:T(4,128)(2,1)S(1)}, bf16[4,16]{1,0:T(4,128)(2,1)S(1)}, u32[]{:S(2)}, u32[]{:S(2)}) %collective-permute-start) | collective-permute-done | bytes 160 | tf_op jit(solution)/shard_map/ppermute | solution.py:20
  88.6 2.9 %collective-permute-done.2 = bf16[4,16,64,256]{3,2,1,0:T(8,128)(2,1)S(1)} collective-permute-done((bf16[4,16,64,256]{3,2,1,0:T(8,128)(2,1)S(1)}, bf16[4,16,64,256]{3,2,1,0:T(8,128)(2,1)S(1)}, u32[]{:S(2)}, u32[]{:S(2)}) %collective-permute-start.2) | collective-permute-done | bytes 2097184 | tf_op jit(solution)/shard_map/ppermute | solution.py:20
  91.5 2.8 %multiply_add_fusion.8 = f32[4,16,64,256]{3,2,1,0:T(8,128)} fusion(bf16[4,16,64,256]{3,2,1,0:T(8,128)(2,1)S(1)} %collective-permute-done.2, f32[4,16,64,256]{3,2,1,0:T(8,128)S(1)} %copy-done, bf16[4,16,64,256]{3,2,1,0:T(8,128)(2,1)S(1)} %collective-permute-done.1, f32[4,16]{1,0:T(4,128)S(1)} %mul.225, f32[4,16]{1,0:T(4,128)S(1)} %convert_multiply_fusion), kind=kLoop, calls=%fused_computation.71 | loop fusion | flops 6291456 | bytes 12583424 | tf_op jit(solution)/shard_map/add | solution.py:83
  94.3 1.9 collective-permute-start.3
  96.2 1.9 collective-permute-start.4
  98.2 1.3 collective-permute-start.6
  99.5 1.9 collective-permute-start.5
  101.4 1.3 collective-permute-start.7
  102.9 1.2 fusion.44
  104.1 4.2 %fusion.32 = f32[4,16,128,64]{2,3,1,0:T(8,128)} fusion(bf16[128,4,16,64]{0,3,2,1:T(8,128)(2,1)S(1)} %bitcast.81, f32[4,128,128]{2,1,0:T(8,128)S(1)} %fusion.44, f32[4,16,128]{2,1,0:T(8,128)} %bitcast.101, f32[4,16,128]{2,1,0:T(8,128)S(1)} %bitcast.103, pred[128,128]{1,0:T(8,128)(4,1)S(1)} %fusion.51), kind=kOutput, calls=%fused_computation.75 | convolution fusion | flops 140509184 | bytes 3489792 | tf_op jit(solution)/shard_map/ghts,sghp->tghp/dot_general | solution.py:53
  109.7 0.9 reshape.555
  110.6 1.6 copy.179
  114.2 1.6 copy.175
  115.8 7.4 %conditional.5 = (f32[4,8,128]{2,1,0:T(8,128)}, f32[4,8,128]{2,1,0:T(8,128)S(1)}, f32[4,8,128,128]{3,2,1,0:T(8,128)S(1)}) conditional(s32[]{:T(128)} %convert_element_type.138, () %tuple.41, (s32[128]{0:T(128)S(1)}, s32[32]{0:T(128)S(1)}, s32[]{:T(128)}, s32[128]{0:T(128)S(1)}, bf16[128,512]{1,0:T(8,128)(2,1)}, ...), branch_computations={%region_6.7_spmd, %region_7.11_spmd} | conditional | flops 272707712 | bytes 18830008 | solution.py:170
  116.0 0.9 reshape.536
  118.1 1.1 fusion.1
  119.9 0.9 reshape.537
  120.9 2.3 %convolution_add_fusion = f32[4,8,128,128]{3,2,1,0:T(8,128)S(1)} fusion(f32[4,8,128,128]{2,3,1,0:T(8,128)} %copy-done.5, f32[4,8,128]{2,1,0:T(8,128)S(1)} %get-tuple-element.383, f32[4,8,128]{2,1,0:T(8,128)} %get-tuple-element.417, bf16[128,4,128,1]{2,1,0,3:T(4,128)(2,1)S(1)} %bitcast.98), kind=kOutput, calls=%fused_computation.4 | convolution fusion | flops 135790592 | bytes 4358144 | tf_op jit(solution)/shard_map/cond/branch_1_fun/ngtk,knd->ngtd/dot_general | solution.py:104
  123.2 25.5 %collective-permute-done.4 = bf16[128,512]{1,0:T(8,128)(2,1)} collective-permute-done((bf16[128,512]{1,0:T(8,128)(2,1)}, bf16[128,512]{1,0:T(8,128)(2,1)}, u32[]{:S(2)}, u32[]{:S(2)}) %collective-permute-start.4) | collective-permute-done | bytes 131104 | tf_op jit(solution)/shard_map/ppermute | solution.py:20
  148.7 1.3 collective-permute-start.8
  150.0 1.5 collective-permute-done.5
  151.5 1.3 collective-permute-start.9
  152.8 1.3 collective-permute-start.10
  154.1 1.3 collective-permute-start.11
  155.4 8.1 %conditional.6 = ((f32[4,8,128]{2,1,0:T(8,128)}, f32[4,8,128]{2,1,0:T(8,128)S(1)}, f32[4,8,128,128]{3,2,1,0:T(8,128)S(1)})) conditional(s32[]{:T(128)} %convert_element_type.137, (f32[4,8,128]{2,1,0:T(8,128)}, f32[4,8,128]{2,1,0:T(8,128)S(1)}, f32[4,8,128,128]{3,2,1,0:T(8,128)S(1)}) %conditional.5, (s32[128]{0:T(128)S(1)}, s32[32]{0:T(128)S(1)}, ...), branch_computations={%region_11.12_spmd, %region_12.16_spmd} | conditional | flops 273223808 | bytes 21009088 | solution.py:170
  155.6 0.9 reshape.538
  159.5 0.9 reshape.539
  160.5 2.4 %multiply_add_fusion = f32[4,8,128,128]{3,2,1,0:T(8,128)S(1)} fusion(f32[4,8,128,128]{3,2,1,0:T(8,128)S(1)} %get-tuple-element.131, f32[4,8,128,128]{2,3,1,0:T(8,128)} %copy-done.1, f32[4,8,128]{2,1,0:T(8,128)S(1)} %get-tuple-element.386, f32[4,8,128]{2,1,0:T(8,128)S(1)} %max.8, bf16[128,4,128,1]{2,1,0,3:T(4,128)(2,1)S(1)} %bitcast.92), kind=kOutput, calls=%fused_computation.16 | convolution fusion | flops 136314880 | bytes 6455296 | tf_op jit(solution)/shard_map/cond/branch_1_fun/ngtk,knd->ngtd/dot_general | solution.py:104
  163.5 8.0 %conditional.7 = ((f32[4,8,128]{2,1,0:T(8,128)}, f32[4,8,128]{2,1,0:T(8,128)S(1)}, f32[4,8,128,128]{3,2,1,0:T(8,128)S(1)})) conditional(s32[]{:T(128)} %convert_element_type.136, (f32[4,8,128]{2,1,0:T(8,128)}, f32[4,8,128]{2,1,0:T(8,128)S(1)}, f32[4,8,128,128]{3,2,1,0:T(8,128)S(1)}) %get-tuple-element.442, (s32[128]{0:T(128)S(1)}, ...), branch_computations={%region_16.17_spmd, %region_17.21_spmd} | conditional | flops 273223808 | bytes 21009088 | solution.py:170
  163.7 0.9 reshape.540
  167.5 0.9 reshape.541
  168.5 2.4 %multiply_add_fusion.2 = f32[4,8,128,128]{3,2,1,0:T(8,128)S(1)} fusion(f32[4,8,128,128]{3,2,1,0:T(8,128)S(1)} %get-tuple-element.141, f32[4,8,128,128]{2,3,1,0:T(8,128)} %copy-done.2, f32[4,8,128]{2,1,0:T(8,128)S(1)} %get-tuple-element.388, f32[4,8,128]{2,1,0:T(8,128)S(1)} %max.9, bf16[128,4,128,1]{2,1,0,3:T(4,128)(2,1)S(1)} %bitcast.94), kind=kOutput, calls=%fused_computation.30 | convolution fusion | flops 136314880 | bytes 6455296 | tf_op jit(solution)/shard_map/cond/branch_1_fun/ngtk,knd->ngtd/dot_general | solution.py:104
  171.5 8.0 %conditional.8 = ((f32[4,8,128]{2,1,0:T(8,128)}, f32[4,8,128]{2,1,0:T(8,128)S(1)}, f32[4,8,128,128]{3,2,1,0:T(8,128)S(1)})) conditional(s32[]{:T(128)} %convert_element_type.135, (f32[4,8,128]{2,1,0:T(8,128)}, f32[4,8,128]{2,1,0:T(8,128)S(1)}, f32[4,8,128,128]{3,2,1,0:T(8,128)S(1)}) %get-tuple-element.443, (s32[128]{0:T(128)S(1)}, ...), branch_computations={%region_21.22_spmd, %region_22.26_spmd} | conditional | flops 273223808 | bytes 21009088 | solution.py:170
  171.7 0.9 reshape.542
  173.1 0.7 max.10
  175.6 0.9 reshape.543
  176.5 2.4 %multiply_add_fusion.4 = f32[4,8,128,128]{3,2,1,0:T(8,128)S(1)} fusion(f32[4,8,128,128]{3,2,1,0:T(8,128)S(1)} %get-tuple-element.151, f32[4,8,128,128]{2,3,1,0:T(8,128)} %copy-done.3, f32[4,8,128]{2,1,0:T(8,128)S(1)} %get-tuple-element.390, f32[4,8,128]{2,1,0:T(8,128)S(1)} %max.10, bf16[128,4,128,1]{2,1,0,3:T(4,128)(2,1)S(1)} %bitcast.96), kind=kOutput, calls=%fused_computation.44 | convolution fusion | flops 136314880 | bytes 6455296 | tf_op jit(solution)/shard_map/cond/branch_1_fun/ngtk,knd->ngtd/dot_general | solution.py:104
  179.5 6.5 %conditional.9 = ((f32[4,8,128]{2,1,0:T(8,128)S(1)}, f32[4,8,128,128]{3,2,1,0:T(8,128)S(1)})) conditional(s32[]{:T(128)} %convert_element_type.134, (f32[4,8,128]{2,1,0:T(8,128)S(1)}, f32[4,8,128,128]{3,2,1,0:T(8,128)S(1)}) %tuple.46, (s32[128]{0:T(128)S(1)}, s32[32]{0:T(128)S(1)}, s32[]{:T(128)}, s32[128]{0:T(128)S(1)}, ...), branch_computations={%region_26.27_spmd, %region_27.31_spmd} | conditional | flops 273223808 | bytes 20976312 | solution.py:170
  180.2 0.7 max.11
  182.7 0.9 reshape.545
  183.7 2.4 %multiply_add_fusion.6 = f32[4,8,128,128]{3,2,1,0:T(8,128)S(1)} fusion(f32[4,8,128,128]{3,2,1,0:T(8,128)S(1)} %get-tuple-element.161, f32[4,8,128,128]{2,3,1,0:T(8,128)} %copy-done.4, f32[4,8,128]{2,1,0:T(8,128)S(1)} %get-tuple-element.392, f32[4,8,128]{2,1,0:T(8,128)S(1)} %max.11, bf16[128,4,128,1]{2,1,0,3:T(4,128)(2,1)S(1)} %bitcast.89), kind=kOutput, calls=%fused_computation.58 | convolution fusion | flops 136314880 | bytes 6455296 | tf_op jit(solution)/shard_map/cond/branch_1_fun/ngtk,knd->ngtd/dot_general | solution.py:104
  187.5 1.3 convert_element_type.141
  188.8 3.6 %all-to-all-start.1 = ((bf16[2,64,4096]{2,1,0:T(8,128)(2,1)}), bf16[2,64,4096]{2,1,0:T(8,128)(2,1)S(1)}, u32[]{:S(2)}, u32[]{:S(2)}) async-start(bf16[2,64,4096]{2,1,0:T(8,128)(2,1)} %convert_element_type.141), calls=%async_computation.1 | async-start | bytes 2097152 | tf_op jit(solution)/shard_map/all_to_all | solution.py:182
  192.4 5.8 %multiply_reduce_fusion = (f32[128,4]{0,1:T(4,128)S(1)}, f32[128,4,16,64]{0,3,2,1:T(8,128)S(1)}) fusion(f32[128,4,16,64]{0,3,2,1:T(8,128)} %bitcast.82, f32[128,4,16]{0,2,1:T(8,128)S(1)} %broadcast_multiply_fusion, f32[4,16,64,256]{3,2,1,0:T(8,128)} %collective-permute-done.3, bf16[128,4,256,1]{2,1,0,3:T(4,128)(2,1)S(1)} %bitcast.99, ...), kind=kOutput, calls=%fused_computation.81 | convolution fusion | flops 1615330816 | bytes 10782720 | tf_op jit(solution)/shard_map/tgn,ghpn->tghp/dot_general | solution.py:72
  198.1 3.7 %reshape.573 = f32[2,64,4096]{1,0,2:T(2,128)} reshape(f32[128,4,16,64]{0,3,2,1:T(8,128)S(1)} %get-tuple-element.413) | data formatting | bytes 4194304 | tf_op jit(solution)/shard_map/reshape | solution.py:75
  201.8 5.3 %copy.233 = f32[2,64,4096]{2,1,0:T(8,128)S(1)} copy(f32[2,64,4096]{1,0,2:T(2,128)} %reshape.573) | data formatting | bytes 4194304 | tf_op jit(solution)/shard_map/reshape | solution.py:75
  207.2 1.7 mul.244
  208.9 3.7 %mul.245 = f32[2,64,4096]{2,1,0:T(8,128)} reshape(f32[128,4,1024]{2,1,0:T(4,128)} %mul.244) | data formatting | bytes 4194304 | tf_op jit(solution)/shard_map/mul | solution.py:79
  212.6 2.8 %multiply_convert_fusion.2 = bf16[2,64,4096]{2,1,0:T(8,128)(2,1)} fusion(f32[2,64,4096]{2,1,0:T(8,128)S(1)} %copy.233, f32[2,64,4096]{2,1,0:T(8,128)} %mul.245, f32[4096]{0:T(1024)S(1)} %copy-done.10), kind=kLoop, calls=%fused_computation.80 | loop fusion | flops 1572864 | bytes 5259264 | tf_op jit(solution)/shard_map/convert_element_type | solution.py:79
  215.4 3.6 %all-to-all-start = ((bf16[2,64,4096]{2,1,0:T(8,128)(2,1)}), bf16[2,64,4096]{2,1,0:T(8,128)(2,1)S(1)}, u32[]{:S(2)}, u32[]{:S(2)}) async-start(bf16[2,64,4096]{2,1,0:T(8,128)(2,1)} %multiply_convert_fusion.2), calls=%async_computation | async-start | bytes 2097152 | tf_op jit(solution)/shard_map/all_to_all | solution.py:181
  219.0 1.1 copy.237
  220.1 8.3 %all-to-all-done = bf16[2,64,4096]{2,1,0:T(8,128)(2,1)S(1)} async-done(((bf16[2,64,4096]{2,1,0:T(8,128)(2,1)}), bf16[2,64,4096]{2,1,0:T(8,128)(2,1)S(1)}, u32[]{:S(2)}, u32[]{:S(2)}) %all-to-all-start) | async-done | bytes 1048608 | tf_op jit(solution)/shard_map/all_to_all | solution.py:181
  228.4 1.1 copy.236
  (99 shorter events, 20.2 us)
Async XLA Ops:
  0.6 9.4 %copy-start.7 = (bf16[128,1024]{1,0:T(8,128)(2,1)S(1)}, bf16[128,1024]{1,0:T(8,128)(2,1)}, u32[]{:S(2)}) copy-start(bf16[128,1024]{1,0:T(8,128)(2,1)} %param.24) | copy-start | bytes 786436
  2.9 4.5 %copy-start.11 = (s32[32]{0:T(128)}, s32[32]{0:T(128)S(1)}, u32[]{:S(2)}) copy-start(s32[32]{0:T(128)S(1)} %get-tuple-element.393) | copy-start | bytes 388
  13.6 27.6 %collective-permute-start.1 = (bf16[4,16,64,256]{3,2,1,0:T(8,128)(2,1)}, bf16[4,16,64,256]{3,2,1,0:T(8,128)(2,1)S(1)}, u32[]{:S(2)}, u32[]{:S(2)}) collective-permute-start(bf16[4,16,64,256]{3,2,1,0:T(8,128)(2,1)} %get-tuple-element.410), channel_id=1, source_target_pairs={{0,2},{2,4},{4,6},{6,8},{8,10},{10,12},{12,14},{14,16},{16,18},{18... | collective-permute-start | bytes 6291464 | tf_op jit(solution)/shard_map/ppermute | solution.py:20
  41.1 50.4 %copy-start = (f32[4,16,64,256]{3,2,1,0:T(8,128)S(1)}, f32[4,16,64,256]{3,2,1,0:T(8,128)}, u32[]{:S(2)}) copy-start(f32[4,16,64,256]{3,2,1,0:T(8,128)} %get-tuple-element.411) | copy-start | bytes 12582916
  44.0 47.5 %collective-permute-start.2 = (bf16[4,16,64,256]{3,2,1,0:T(8,128)(2,1)S(1)}, bf16[4,16,64,256]{3,2,1,0:T(8,128)(2,1)S(1)}, u32[]{:S(2)}, u32[]{:S(2)}) collective-permute-start(bf16[4,16,64,256]{3,2,1,0:T(8,128)(2,1)S(1)} %fusion.31), channel_id=1, source_target_pairs={{0,4},{2,6},{4,8},{6,10},{8,12},{10,14},{12,16},{14,18},{16,20},{1... | collective-permute-start | bytes 6291464 | tf_op jit(solution)/shard_map/ppermute | solution.py:20
  45.3 43.2 %collective-permute-start = (bf16[4,16]{1,0:T(4,128)(2,1)S(1)}, bf16[4,16]{1,0:T(4,128)(2,1)S(1)}, u32[]{:S(2)}, u32[]{:S(2)}) collective-permute-start(bf16[4,16]{1,0:T(4,128)(2,1)S(1)} %convert_element_type.121), channel_id=1, source_target_pairs={{0,2},{2,4},{4,6},{6,8},{8,10},{10,12},{12,14},{14,16},{16,18},{18... | collective-permute-start | bytes 392 | tf_op jit(solution)/shard_map/ppermute | solution.py:20
  94.3 98.0 %collective-permute-start.3 = (f32[4,16,64,256]{3,2,1,0:T(8,128)}, f32[4,16,64,256]{3,2,1,0:T(8,128)}, u32[]{:S(2)}, u32[]{:S(2)}) collective-permute-start(f32[4,16,64,256]{3,2,1,0:T(8,128)} %multiply_add_fusion.8), channel_id=1, source_target_pairs={{0,2},{2,4},{4,6},{6,8},{8,10},{10,12},{12,14},{14,16},{16,18},{18... | collective-permute-start | bytes 12582920 | tf_op jit(solution)/shard_map/ppermute | solution.py:20
  96.2 52.4 %collective-permute-start.4 = (bf16[128,512]{1,0:T(8,128)(2,1)}, bf16[128,512]{1,0:T(8,128)(2,1)}, u32[]{:S(2)}, u32[]{:S(2)}) collective-permute-start(bf16[128,512]{1,0:T(8,128)(2,1)} %param.30), channel_id=1, source_target_pairs={{0,2},{2,4},{4,6},{6,8},{8,10},{10,12},{12,14},{14,16},{16,18},{18... | collective-permute-start | bytes 393224 | tf_op jit(solution)/shard_map/ppermute | solution.py:20
  98.2 54.6 %collective-permute-start.6 = (bf16[128,512]{1,0:T(8,128)(2,1)}, bf16[128,512]{1,0:T(8,128)(2,1)}, u32[]{:S(2)}, u32[]{:S(2)}) collective-permute-start(bf16[128,512]{1,0:T(8,128)(2,1)} %param.30), channel_id=1, source_target_pairs={{0,4},{2,6},{4,8},{6,10},{8,12},{10,14},{12,16},{14,18},{16,20},{1... | collective-permute-start | bytes 393224 | tf_op jit(solution)/shard_map/ppermute | solution.py:20
  99.5 52.0 %collective-permute-start.5 = (bf16[128,512]{1,0:T(8,128)(2,1)}, bf16[128,512]{1,0:T(8,128)(2,1)}, u32[]{:S(2)}, u32[]{:S(2)}) collective-permute-start(bf16[128,512]{1,0:T(8,128)(2,1)} %param.31), channel_id=1, source_target_pairs={{0,2},{2,4},{4,6},{6,8},{8,10},{10,12},{12,14},{14,16},{16,18},{18... | collective-permute-start | bytes 393224 | tf_op jit(solution)/shard_map/ppermute | solution.py:20
  101.4 52.7 %collective-permute-start.7 = (bf16[128,512]{1,0:T(8,128)(2,1)}, bf16[128,512]{1,0:T(8,128)(2,1)}, u32[]{:S(2)}, u32[]{:S(2)}) collective-permute-start(bf16[128,512]{1,0:T(8,128)(2,1)} %param.31), channel_id=1, source_target_pairs={{0,4},{2,6},{4,8},{6,10},{8,12},{10,14},{12,16},{14,18},{16,20},{1... | collective-permute-start | bytes 393224 | tf_op jit(solution)/shard_map/ppermute | solution.py:20
  104.1 5.6 %copy-start.8 = (bf16[128,1024]{1,0:T(8,128)(2,1)S(1)}, bf16[128,1024]{1,0:T(8,128)(2,1)}, u32[]{:S(2)}) copy-start(bf16[128,1024]{1,0:T(8,128)(2,1)} %param.25) | copy-start | bytes 786436
  108.3 6.0 %copy-start.6 = (bf16[128,4096]{1,0:T(8,128)(2,1)S(1)}, bf16[128,4096]{1,0:T(8,128)(2,1)}, u32[]{:S(2)}) copy-start(bf16[128,4096]{1,0:T(8,128)(2,1)} %param.23) | copy-start | bytes 3145732
  108.3 6.0 %copy-start.12 = (s32[32]{0:T(128)S(1)}, s32[32]{0:T(128)}, u32[]{:S(2)}) copy-start(s32[32]{0:T(128)} %copy-done.11) | copy-start | bytes 388
  117.4 3.5 %copy-start.5 = (f32[4,8,128,128]{2,3,1,0:T(8,128)}, f32[4,8,128,128]{2,3,1,0:T(8,128)S(1)}, u32[]{:S(2)}) copy-start(f32[4,8,128,128]{2,3,1,0:T(8,128)S(1)} %get-tuple-element.395) | copy-start | bytes 6291460 | tf_op jit(solution)/shard_map/cond
  148.7 22.8 %collective-permute-start.8 = (bf16[128,512]{1,0:T(8,128)(2,1)}, bf16[128,512]{1,0:T(8,128)(2,1)}, u32[]{:S(2)}, u32[]{:S(2)}) collective-permute-start(bf16[128,512]{1,0:T(8,128)(2,1)} %param.30), channel_id=1, source_target_pairs={{0,6},{2,8},{4,10},{6,12},{8,14},{10,16},{12,18},{14,20},{16,22},{... | collective-permute-start | bytes 393224 | tf_op jit(solution)/shard_map/ppermute | solution.py:20
  151.5 20.0 %collective-permute-start.9 = (bf16[128,512]{1,0:T(8,128)(2,1)}, bf16[128,512]{1,0:T(8,128)(2,1)}, u32[]{:S(2)}, u32[]{:S(2)}) collective-permute-start(bf16[128,512]{1,0:T(8,128)(2,1)} %param.31), channel_id=1, source_target_pairs={{0,6},{2,8},{4,10},{6,12},{8,14},{10,16},{12,18},{14,20},{16,22},{... | collective-permute-start | bytes 393224 | tf_op jit(solution)/shard_map/ppermute | solution.py:20
  152.8 26.7 %collective-permute-start.10 = (bf16[128,512]{1,0:T(8,128)(2,1)}, bf16[128,512]{1,0:T(8,128)(2,1)S(1)}, u32[]{:S(2)}, u32[]{:S(2)}) collective-permute-start(bf16[128,512]{1,0:T(8,128)(2,1)} %param.30), channel_id=1, source_target_pairs={{0,8},{2,10},{4,12},{6,14},{8,16},{10,18},{12,20},{14,22},{16,24},... | collective-permute-start | bytes 393224 | tf_op jit(solution)/shard_map/ppermute | solution.py:20
  154.1 25.4 %collective-permute-start.11 = (bf16[128,512]{1,0:T(8,128)(2,1)}, bf16[128,512]{1,0:T(8,128)(2,1)}, u32[]{:S(2)}, u32[]{:S(2)}) collective-permute-start(bf16[128,512]{1,0:T(8,128)(2,1)} %param.31), channel_id=1, source_target_pairs={{0,8},{2,10},{4,12},{6,14},{8,16},{10,18},{12,20},{14,22},{16,24},... | collective-permute-start | bytes 393224 | tf_op jit(solution)/shard_map/ppermute | solution.py:20
  157.0 1.4 copy-start.1
  165.0 1.4 copy-start.2
  173.1 1.4 copy-start.3
  180.2 1.4 copy-start.4
  187.5 4.9 %copy-start.9 = (bf16[128,4,256]{2,1,0:T(4,128)(2,1)S(1)}, bf16[128,4,256]{2,1,0:T(4,128)(2,1)}, u32[]{:S(2)}) copy-start(bf16[128,4,256]{2,1,0:T(4,128)(2,1)} %reshape.555) | copy-start | bytes 786436
  188.8 26.7 %all-to-all-start.1 = ((bf16[2,64,4096]{2,1,0:T(8,128)(2,1)}), bf16[2,64,4096]{2,1,0:T(8,128)(2,1)S(1)}, u32[]{:S(2)}, u32[]{:S(2)}) async-start(bf16[2,64,4096]{2,1,0:T(8,128)(2,1)} %convert_element_type.141), calls=%async_computation.1 | async-start | bytes 2097152 | tf_op jit(solution)/shard_map/all_to_all | solution.py:182
  208.9 3.7 %copy-start.10 = (f32[4096]{0:T(1024)S(1)}, f32[4096]{0:T(1024)}, u32[]{:S(2)}) copy-start(f32[4096]{0:T(1024)} %param.28) | copy-start | bytes 49156
  215.4 13.0 %all-to-all-start = ((bf16[2,64,4096]{2,1,0:T(8,128)(2,1)}), bf16[2,64,4096]{2,1,0:T(8,128)(2,1)S(1)}, u32[]{:S(2)}, u32[]{:S(2)}) async-start(bf16[2,64,4096]{2,1,0:T(8,128)(2,1)} %multiply_convert_fusion.2), calls=%async_computation | async-start | bytes 2097152 | tf_op jit(solution)/shard_map/all_to_all | solution.py:181
where the time goes:
time: 231 us; the launch traced here: 229 us
  waiting for transfers between devices  104 us (45%)
  local copies, waits for them, and re-layouts  40.5 us (18%)
  matrix products  28.5 us (12%)
  starting transfers between devices  25.8 us (11%)
  other arithmetic  24.3 us (11%)
  between operations  5.7 us (2%)
    ppermute x12, waiting for transfers between devices, passed_along(): return lax.ppermute(block, axis, route)  96.1 us
    ppermute x12, starting transfers between devices, passed_along(): return lax.ppermute(block, axis, route)  18.6 us
    dot_general x5, matrix products, attention_update(): jnp.einsum('ngtk,knd->ngtd', probs.astype(jnp.bfloat16), value_heads, pre...  11.8 us
    reshape x2, local copies, waits for them, and re-layouts, finish_rows(): (mixer_out * jax.nn.silu(gate_vals)).reshape(tok_rows, group_count, group...  8.96 us
    all_to_all x1, waiting for transfers between devices, local(): lax.all_to_all(mixed_rows, 'tp', split_axis=0, concat_axis=1, tiled=True)  8.3 us
    dot_general x1, matrix products, finish_rows(): jnp.einsum('tgn,ghpn->tghp', out_proj, carried, precision=lax.Precision.H...  5.78 us
    mul x2, local copies, waits for them, and re-layouts, finish_rows(): gated * factor  5.36 us
    reshape x5, local copies, waits for them, and re-layouts, attention_update(): value_heads = value_block.reshape(block_rows, kv_local, ATT_DIM)  4.7 us
  transfers between devices with their start and end apart: 14, of which 6 were waited for; matrix products, arithmetic and copies ran while one was open for 32% of the time, Pallas kernels for 0%

commit v1 on v0

--- a/solution.py
+++ b/solution.py
@@ -8,6 +8,12 @@
 ATT_DIM = 128
 DOC_DEVS = 4
 NEG_LARGE = -1e30
+
+
+def exchange_blocks(shard, axis, split, join):
+    cells = jnp.split(shard, lax.axis_size(axis), axis=split)
+    received = lax.all_to_all(jnp.stack(cells), axis, 0, 0)
+    return jnp.concatenate(received, axis=join)
 
 
 def for_sending(x):
@@ -178,7 +184,7 @@
         jnp.transpose(final_out, (2, 0, 1, 3)).reshape(tok_rows, -1).astype(jnp.bfloat16)
     )
     mixed_local, attended_local = (
-        lax.all_to_all(mixed_rows, "tp", split_axis=0, concat_axis=1, tiled=True),
+        exchange_blocks(mixed_rows, "tp", 0, 1),
         lax.all_to_all(attended_rows, "tp", split_axis=0, concat_axis=1, tiled=True),
     )
     return (mixed_local, attended_local)

time: 231 us -> 223 us (0.965)
  local copies, waits for them, and re-layouts: 40.5 us -> 31.8 us
    reshape x2 -> x1, local copies, waits for them, and re-layouts: 8.96 us -> 2.92 us  [finish_rows(): (mixer_out * jax.nn.silu(gate_vals)).reshape(tok_rows, group_count, group...]
    mul x2 -> x1, local copies, waits for them, and re-layouts: 5.36 us -> 0.34 us  [finish_rows(): gated * factor]
    unnamed x19 -> x22, local copies, waits for them, and re-layouts: 4.14 us -> 5.79 us
  transfers between devices with their start and end apart: 14 -> 14, of which waited for: 6 -> 6; matrix products, arithmetic and copies ran while one was open for 32% -> 29% of each run, Pallas kernels for 0% -> 0%
where the time goes in v1:
time: 223 us; the launch traced here: 221 us
  waiting for transfers between devices  104 us (47%)
  local copies, waits for them, and re-layouts  31.8 us (14%)
  matrix products  29.3 us (13%)
  starting transfers between devices  25.9 us (12%)
  other arithmetic  24.4 us (11%)
  between operations  5.73 us (3%)
    ppermute x12, waiting for transfers between devices, passed_along(): return lax.ppermute(block, axis, route)  95.4 us
    ppermute x12, starting transfers between devices, passed_along(): return lax.ppermute(block, axis, route)  18.6 us
    dot_general x5, matrix products, attention_update(): jnp.einsum('ngtk,knd->ngtd', probs.astype(jnp.bfloat16), value_heads, pre...  11.8 us
    all_to_all x1, waiting for transfers between devices, exchange_blocks(): received = lax.all_to_all(jnp.stack(cells), axis, 0, 0)  8.33 us
    dot_general x1, matrix products, finish_rows(): jnp.einsum('tgn,ghpn->tghp', out_proj, carried, precision=lax.Precision.H...  6.59 us
    unnamed x22, local copies, waits for them, and re-layouts  5.79 us
    cond x13, local copies, waits for them, and re-layouts  4.93 us
    reshape x5, local copies, waits for them, and re-layouts, attention_update(): value_heads = value_block.reshape(block_rows, kv_local, ATT_DIM)  4.7 us
  transfers between devices with their start and end apart: 14, of which 6 were waited for; matrix products, arithmetic and copies ran while one was open for 29% of the time, Pallas kernels for 0%

profile of v1, /device:TPU:26, one launch (start us, length us, event | category | flops | bytes accessed | tf_op | source)
XLA Modules:
  0.0 221.2 jit_solution(10508418064444422161)
XLA Ops:
  0.7 0.8 copy.236
  1.6 1.3 fusion.53
  5.7 0.8 copy.242
  6.6 0.8 multiply_negate_fusion
  8.4 1.6 copy.241
  10.2 3.4 %fusion.61 = (bf16[4,16,64,256]{3,2,1,0:T(8,128)(2,1)}, f32[4,16,64,256]{3,2,1,0:T(8,128)}) fusion(bf16[128,4,256,1]{2,1,0,3:T(4,128)(2,1)S(1)} %bitcast.93, bf16[128,4,16,64]{0,3,2,1:T(8,128)(2,1)S(1)} %bitcast.85, f32[128,4,16]{0,2,1:T(8,128)S(1)} %bitcast.106), kind=kOutput, calls=%fused_computation.127 | convolution fusion | flops 271056896 | bytes 7634944 | tf_op jit(solution)/shard_map/sghp,sgn->ghpn/dot_general | solution.py:69
  13.6 1.9 collective-permute-start.1
  16.2 24.9 %collective-permute-done.1 = bf16[4,16,64,256]{3,2,1,0:T(8,128)(2,1)S(1)} collective-permute-done((bf16[4,16,64,256]{3,2,1,0:T(8,128)(2,1)}, bf16[4,16,64,256]{3,2,1,0:T(8,128)(2,1)S(1)}, u32[]{:S(2)}, u32[]{:S(2)}) %collective-permute-start.1) | collective-permute-done | bytes 2097184 | tf_op jit(solution)/shard_map/ppermute | solution.py:26
  41.1 2.9 %fusion.31 = bf16[4,16,64,256]{3,2,1,0:T(8,128)(2,1)S(1)} fusion(f32[4,16,64,256]{3,2,1,0:T(8,128)} %get-tuple-element.507, bf16[4,16,64,256]{3,2,1,0:T(8,128)(2,1)S(1)} %collective-permute-done.1, f32[4,16]{1,0:T(4,128)S(1)} %mul.223), kind=kLoop, calls=%fused_computation.74 | loop fusion | flops 4194304 | bytes 8388864 | tf_op jit(solution)/shard_map/convert_element_type | solution.py:20
  44.0 1.3 collective-permute-start.2
  45.3 1.9 collective-permute-start
  47.2 41.3 %collective-permute-done = bf16[4,16]{1,0:T(4,128)(2,1)S(1)} collective-permute-done((bf16[4,16]{1,0:T(4,128)(2,1)S(1)}, bf16[4,16]{1,0:T(4,128)(2,1)S(1)}, u32[]{:S(2)}, u32[]{:S(2)}) %collective-permute-start) | collective-permute-done | bytes 160 | tf_op jit(solution)/shard_map/ppermute | solution.py:26
  88.6 2.9 %collective-permute-done.2 = bf16[4,16,64,256]{3,2,1,0:T(8,128)(2,1)S(1)} collective-permute-done((bf16[4,16,64,256]{3,2,1,0:T(8,128)(2,1)S(1)}, bf16[4,16,64,256]{3,2,1,0:T(8,128)(2,1)S(1)}, u32[]{:S(2)}, u32[]{:S(2)}) %collective-permute-start.2) | collective-permute-done | bytes 2097184 | tf_op jit(solution)/shard_map/ppermute | solution.py:26
  91.5 2.9 %multiply_add_fusion.8 = f32[4,16,64,256]{3,2,1,0:T(8,128)} fusion(bf16[4,16,64,256]{3,2,1,0:T(8,128)(2,1)S(1)} %collective-permute-done.2, f32[4,16,64,256]{3,2,1,0:T(8,128)S(1)} %copy-done, bf16[4,16,64,256]{3,2,1,0:T(8,128)(2,1)S(1)} %collective-permute-done.1, f32[4,16]{1,0:T(4,128)S(1)} %mul.223, f32[4,16]{1,0:T(4,128)S(1)} %convert_multiply_fusion), kind=kLoop, calls=%fused_computation.71 | loop fusion | flops 6291456 | bytes 12583424 | tf_op jit(solution)/shard_map/add | solution.py:89
  94.4 1.9 collective-permute-start.3
  96.3 1.9 collective-permute-start.4
  98.2 1.3 collective-permute-start.6
  99.5 1.9 collective-permute-start.5
  101.5 1.3 collective-permute-start.7
  102.9 1.2 fusion.44
  104.1 4.2 %fusion.32 = f32[4,16,128,64]{2,3,1,0:T(8,128)} fusion(bf16[128,4,16,64]{0,3,2,1:T(8,128)(2,1)S(1)} %bitcast.86, f32[4,128,128]{2,1,0:T(8,128)S(1)} %fusion.44, f32[4,16,128]{2,1,0:T(8,128)} %bitcast.107, f32[4,16,128]{2,1,0:T(8,128)S(1)} %bitcast.109, pred[128,128]{1,0:T(8,128)(4,1)S(1)} %fusion.51), kind=kOutput, calls=%fused_computation.75 | convolution fusion | flops 140509184 | bytes 3489792 | tf_op jit(solution)/shard_map/ghts,sghp->tghp/dot_general | solution.py:59
  109.7 0.9 reshape.551
  110.6 1.6 copy.251
  114.3 1.6 copy.247
  115.9 8.0 %conditional.5 = (f32[4,8,128]{2,1,0:T(8,128)}, f32[4,8,128]{2,1,0:T(8,128)S(1)}, f32[4,8,128,128]{3,2,1,0:T(8,128)S(1)}) conditional(s32[]{:T(128)} %convert_element_type.137, () %tuple.41, (s32[128]{0:T(128)S(1)}, s32[32]{0:T(128)S(1)}, s32[]{:T(128)}, s32[128]{0:T(128)S(1)}, bf16[128,512]{1,0:T(8,128)(2,1)}, ...), branch_computations={%region_6.7_spmd, %region_7.11_spmd} | conditional | flops 272707712 | bytes 18830008 | solution.py:176
  116.1 0.9 reshape.530
  118.8 1.1 fusion.1
  120.7 0.9 reshape.531
  121.6 2.3 %convolution_add_fusion = f32[4,8,128,128]{3,2,1,0:T(8,128)S(1)} fusion(f32[4,8,128,128]{2,3,1,0:T(8,128)} %copy-done.5, f32[4,8,128]{2,1,0:T(8,128)S(1)} %get-tuple-element.477, f32[4,8,128]{2,1,0:T(8,128)} %get-tuple-element.513, bf16[128,4,128,1]{2,1,0,3:T(4,128)(2,1)S(1)} %bitcast.104), kind=kOutput, calls=%fused_computation.4 | convolution fusion | flops 135790592 | bytes 4358144 | tf_op jit(solution)/shard_map/cond/branch_1_fun/ngtk,knd->ngtd/dot_general | solution.py:110
  123.9 24.8 %collective-permute-done.4 = bf16[128,512]{1,0:T(8,128)(2,1)} collective-permute-done((bf16[128,512]{1,0:T(8,128)(2,1)}, bf16[128,512]{1,0:T(8,128)(2,1)}, u32[]{:S(2)}, u32[]{:S(2)}) %collective-permute-start.4) | collective-permute-done | bytes 131104 | tf_op jit(solution)/shard_map/ppermute | solution.py:26
  148.7 1.3 collective-permute-start.8
  150.0 1.5 collective-permute-done.5
  151.5 1.3 collective-permute-start.9
  152.8 1.3 collective-permute-start.10
  154.1 1.3 collective-permute-start.11
  155.4 8.1 %conditional.6 = ((f32[4,8,128]{2,1,0:T(8,128)}, f32[4,8,128]{2,1,0:T(8,128)S(1)}, f32[4,8,128,128]{3,2,1,0:T(8,128)S(1)})) conditional(s32[]{:T(128)} %convert_element_type.136, (f32[4,8,128]{2,1,0:T(8,128)}, f32[4,8,128]{2,1,0:T(8,128)S(1)}, f32[4,8,128,128]{3,2,1,0:T(8,128)S(1)}) %conditional.5, (s32[128]{0:T(128)S(1)}, s32[32]{0:T(128)S(1)}, ...), branch_computations={%region_11.12_spmd, %region_12.16_spmd} | conditional | flops 273223808 | bytes 21009088 | solution.py:176
  155.7 0.9 reshape.532
  157.1 0.7 max.8
  159.6 0.9 reshape.533
  160.5 2.4 %multiply_add_fusion = f32[4,8,128,128]{3,2,1,0:T(8,128)S(1)} fusion(f32[4,8,128,128]{3,2,1,0:T(8,128)S(1)} %get-tuple-element.131, f32[4,8,128,128]{2,3,1,0:T(8,128)} %copy-done.1, f32[4,8,128]{2,1,0:T(8,128)S(1)} %get-tuple-element.480, f32[4,8,128]{2,1,0:T(8,128)S(1)} %max.8, bf16[128,4,128,1]{2,1,0,3:T(4,128)(2,1)S(1)} %bitcast.98), kind=kOutput, calls=%fused_computation.16 | convolution fusion | flops 136314880 | bytes 6455296 | tf_op jit(solution)/shard_map/cond/branch_1_fun/ngtk,knd->ngtd/dot_general | solution.py:110
  163.5 8.0 %conditional.7 = ((f32[4,8,128]{2,1,0:T(8,128)}, f32[4,8,128]{2,1,0:T(8,128)S(1)}, f32[4,8,128,128]{3,2,1,0:T(8,128)S(1)})) conditional(s32[]{:T(128)} %convert_element_type.135, (f32[4,8,128]{2,1,0:T(8,128)}, f32[4,8,128]{2,1,0:T(8,128)S(1)}, f32[4,8,128,128]{3,2,1,0:T(8,128)S(1)}) %get-tuple-element.538, (s32[128]{0:T(128)S(1)}, ...), branch_computations={%region_16.17_spmd, %region_17.21_spmd} | conditional | flops 273223808 | bytes 21009088 | solution.py:176
  163.7 0.9 reshape.534
  165.1 0.7 max.9
  167.6 0.9 reshape.535
  168.5 2.4 %multiply_add_fusion.2 = f32[4,8,128,128]{3,2,1,0:T(8,128)S(1)} fusion(f32[4,8,128,128]{3,2,1,0:T(8,128)S(1)} %get-tuple-element.141, f32[4,8,128,128]{2,3,1,0:T(8,128)} %copy-done.2, f32[4,8,128]{2,1,0:T(8,128)S(1)} %get-tuple-element.482, f32[4,8,128]{2,1,0:T(8,128)S(1)} %max.9, bf16[128,4,128,1]{2,1,0,3:T(4,128)(2,1)S(1)} %bitcast.100), kind=kOutput, calls=%fused_computation.30 | convolution fusion | flops 136314880 | bytes 6455296 | tf_op jit(solution)/shard_map/cond/branch_1_fun/ngtk,knd->ngtd/dot_general | solution.py:110
  171.5 8.0 %conditional.8 = ((f32[4,8,128]{2,1,0:T(8,128)}, f32[4,8,128]{2,1,0:T(8,128)S(1)}, f32[4,8,128,128]{3,2,1,0:T(8,128)S(1)})) conditional(s32[]{:T(128)} %convert_element_type.134, (f32[4,8,128]{2,1,0:T(8,128)}, f32[4,8,128]{2,1,0:T(8,128)S(1)}, f32[4,8,128,128]{3,2,1,0:T(8,128)S(1)}) %get-tuple-element.539, (s32[128]{0:T(128)S(1)}, ...), branch_computations={%region_21.22_spmd, %region_22.26_spmd} | conditional | flops 273223808 | bytes 21009088 | solution.py:176
  171.8 0.9 reshape.536
  173.1 0.7 max.10
  175.6 0.9 reshape.537
  176.6 2.4 %multiply_add_fusion.4 = f32[4,8,128,128]{3,2,1,0:T(8,128)S(1)} fusion(f32[4,8,128,128]{3,2,1,0:T(8,128)S(1)} %get-tuple-element.151, f32[4,8,128,128]{2,3,1,0:T(8,128)} %copy-done.3, f32[4,8,128]{2,1,0:T(8,128)S(1)} %get-tuple-element.484, f32[4,8,128]{2,1,0:T(8,128)S(1)} %max.10, bf16[128,4,128,1]{2,1,0,3:T(4,128)(2,1)S(1)} %bitcast.102), kind=kOutput, calls=%fused_computation.44 | convolution fusion | flops 136314880 | bytes 6455296 | tf_op jit(solution)/shard_map/cond/branch_1_fun/ngtk,knd->ngtd/dot_general | solution.py:110
  179.6 6.5 %conditional.9 = ((f32[4,8,128]{2,1,0:T(8,128)S(1)}, f32[4,8,128,128]{3,2,1,0:T(8,128)S(1)})) conditional(s32[]{:T(128)} %convert_element_type.133, (f32[4,8,128]{2,1,0:T(8,128)S(1)}, f32[4,8,128,128]{3,2,1,0:T(8,128)S(1)}) %tuple.46, (s32[128]{0:T(128)S(1)}, s32[32]{0:T(128)S(1)}, s32[]{:T(128)}, s32[128]{0:T(128)S(1)}, ...), branch_computations={%region_26.27_spmd, %region_27.31_spmd} | conditional | flops 273223808 | bytes 20976312 | solution.py:176
  182.8 0.9 reshape.539
  183.7 2.4 %multiply_add_fusion.6 = f32[4,8,128,128]{3,2,1,0:T(8,128)S(1)} fusion(f32[4,8,128,128]{3,2,1,0:T(8,128)S(1)} %get-tuple-element.161, f32[4,8,128,128]{2,3,1,0:T(8,128)} %copy-done.4, f32[4,8,128]{2,1,0:T(8,128)S(1)} %get-tuple-element.486, f32[4,8,128]{2,1,0:T(8,128)S(1)} %max.11, bf16[128,4,128,1]{2,1,0,3:T(4,128)(2,1)S(1)} %bitcast.95), kind=kOutput, calls=%fused_computation.58 | convolution fusion | flops 136314880 | bytes 6455296 | tf_op jit(solution)/shard_map/cond/branch_1_fun/ngtk,knd->ngtd/dot_general | solution.py:110
  187.5 1.3 convert_element_type.140
  188.8 3.7 %all-to-all-start.1 = ((bf16[2,64,4096]{2,1,0:T(8,128)(2,1)}), bf16[2,64,4096]{2,1,0:T(8,128)(2,1)S(1)}, u32[]{:S(2)}, u32[]{:S(2)}) async-start(bf16[2,64,4096]{2,1,0:T(8,128)(2,1)} %convert_element_type.140), calls=%async_computation.1 | async-start | bytes 2097152 | tf_op jit(solution)/shard_map/all_to_all | solution.py:188
  192.6 6.6 %multiply_reduce_fusion = (f32[128,4]{0,1:T(4,128)S(1)}, f32[128,4,16,64]{0,3,2,1:T(8,128)}) fusion(f32[128,4,16,64]{0,3,2,1:T(8,128)S(1)} %bitcast.87, f32[128,4,16]{0,2,1:T(8,128)S(1)} %broadcast_multiply_fusion, f32[4,16,64,256]{3,2,1,0:T(8,128)} %collective-permute-done.3, bf16[128,4,256,1]{2,1,0,3:T(4,128)(2,1)S(1)} %bitcast.105, ...), kind=kOutput, calls=%fused_computation.81 | convolution fusion | flops 1615330816 | bytes 10782720 | tf_op jit(solution)/shard_map/tgn,ghpn->tghp/dot_general | solution.py:78
  199.6 1.6 copy.309
  201.3 2.9 %copy.249 = f32[128,4096]{1,0:T(8,128)} copy(f32[128,4096]{0,1:T(8,128)} %bitcast.88) | data formatting | bytes 4194304 | tf_op jit(solution)/shard_map/reshape | solution.py:81
  204.2 1.8 multiply_convert_fusion.2
  206.1 1.1 pad_maximum_fusion
  207.2 3.6 %all-to-all-start = ((bf16[2,64,4096]{2,1,0:T(8,128)(2,1)}), bf16[2,64,4096]{2,1,0:T(8,128)(2,1)S(1)}, u32[]{:S(2)}, u32[]{:S(2)}) async-start(bf16[2,64,4096]{2,1,0:T(8,128)(2,1)} %pad_maximum_fusion), calls=%async_computation | async-start | bytes 2097152 | tf_op jit(solution)/shard_map/all_to_all | solution.py:15
  210.8 1.0 copy.308
  211.8 8.3 %all-to-all-done = bf16[2,64,4096]{2,1,0:T(8,128)(2,1)S(1)} async-done(((bf16[2,64,4096]{2,1,0:T(8,128)(2,1)}), bf16[2,64,4096]{2,1,0:T(8,128)(2,1)S(1)}, u32[]{:S(2)}, u32[]{:S(2)}) %all-to-all-start) | async-done | bytes 1048608 | tf_op jit(solution)/shard_map/all_to_all | solution.py:15
  220.1 1.0 copy.307
  (102 shorter events, 20.6 us)
Async XLA Ops:
  0.6 9.4 %copy-start.8 = (bf16[128,1024]{1,0:T(8,128)(2,1)S(1)}, bf16[128,1024]{1,0:T(8,128)(2,1)}, u32[]{:S(2)}) copy-start(bf16[128,1024]{1,0:T(8,128)(2,1)} %param.24) | copy-start | bytes 786436
  2.9 4.5 %copy-start.12 = (s32[32]{0:T(128)}, s32[32]{0:T(128)S(1)}, u32[]{:S(2)}) copy-start(s32[32]{0:T(128)S(1)} %get-tuple-element.487) | copy-start | bytes 388
  13.6 27.6 %collective-permute-start.1 = (bf16[4,16,64,256]{3,2,1,0:T(8,128)(2,1)}, bf16[4,16,64,256]{3,2,1,0:T(8,128)(2,1)S(1)}, u32[]{:S(2)}, u32[]{:S(2)}) collective-permute-start(bf16[4,16,64,256]{3,2,1,0:T(8,128)(2,1)} %get-tuple-element.506), channel_id=1, source_target_pairs={{0,2},{2,4},{4,6},{6,8},{8,10},{10,12},{12,14},{14,16},{16,18},{18... | collective-permute-start | bytes 6291464 | tf_op jit(solution)/shard_map/ppermute | solution.py:26
  41.1 50.4 %copy-start = (f32[4,16,64,256]{3,2,1,0:T(8,128)S(1)}, f32[4,16,64,256]{3,2,1,0:T(8,128)}, u32[]{:S(2)}) copy-start(f32[4,16,64,256]{3,2,1,0:T(8,128)} %get-tuple-element.507) | copy-start | bytes 12582916
  44.0 47.5 %collective-permute-start.2 = (bf16[4,16,64,256]{3,2,1,0:T(8,128)(2,1)S(1)}, bf16[4,16,64,256]{3,2,1,0:T(8,128)(2,1)S(1)}, u32[]{:S(2)}, u32[]{:S(2)}) collective-permute-start(bf16[4,16,64,256]{3,2,1,0:T(8,128)(2,1)S(1)} %fusion.31), channel_id=1, source_target_pairs={{0,4},{2,6},{4,8},{6,10},{8,12},{10,14},{12,16},{14,18},{16,20},{1... | collective-permute-start | bytes 6291464 | tf_op jit(solution)/shard_map/ppermute | solution.py:26
  45.3 43.2 %collective-permute-start = (bf16[4,16]{1,0:T(4,128)(2,1)S(1)}, bf16[4,16]{1,0:T(4,128)(2,1)S(1)}, u32[]{:S(2)}, u32[]{:S(2)}) collective-permute-start(bf16[4,16]{1,0:T(4,128)(2,1)S(1)} %convert_element_type.120), channel_id=1, source_target_pairs={{0,2},{2,4},{4,6},{6,8},{8,10},{10,12},{12,14},{14,16},{16,18},{18... | collective-permute-start | bytes 392 | tf_op jit(solution)/shard_map/ppermute | solution.py:26
  94.4 98.2 %collective-permute-start.3 = (f32[4,16,64,256]{3,2,1,0:T(8,128)}, f32[4,16,64,256]{3,2,1,0:T(8,128)}, u32[]{:S(2)}, u32[]{:S(2)}) collective-permute-start(f32[4,16,64,256]{3,2,1,0:T(8,128)} %multiply_add_fusion.8), channel_id=1, source_target_pairs={{0,2},{2,4},{4,6},{6,8},{8,10},{10,12},{12,14},{14,16},{16,18},{18... | collective-permute-start | bytes 12582920 | tf_op jit(solution)/shard_map/ppermute | solution.py:26
  96.3 52.4 %collective-permute-start.4 = (bf16[128,512]{1,0:T(8,128)(2,1)}, bf16[128,512]{1,0:T(8,128)(2,1)}, u32[]{:S(2)}, u32[]{:S(2)}) collective-permute-start(bf16[128,512]{1,0:T(8,128)(2,1)} %param.30), channel_id=1, source_target_pairs={{0,2},{2,4},{4,6},{6,8},{8,10},{10,12},{12,14},{14,16},{16,18},{18... | collective-permute-start | bytes 393224 | tf_op jit(solution)/shard_map/ppermute | solution.py:26
  98.2 54.6 %collective-permute-start.6 = (bf16[128,512]{1,0:T(8,128)(2,1)}, bf16[128,512]{1,0:T(8,128)(2,1)}, u32[]{:S(2)}, u32[]{:S(2)}) collective-permute-start(bf16[128,512]{1,0:T(8,128)(2,1)} %param.30), channel_id=1, source_target_pairs={{0,4},{2,6},{4,8},{6,10},{8,12},{10,14},{12,16},{14,18},{16,20},{1... | collective-permute-start | bytes 393224 | tf_op jit(solution)/shard_map/ppermute | solution.py:26
  99.5 52.0 %collective-permute-start.5 = (bf16[128,512]{1,0:T(8,128)(2,1)}, bf16[128,512]{1,0:T(8,128)(2,1)}, u32[]{:S(2)}, u32[]{:S(2)}) collective-permute-start(bf16[128,512]{1,0:T(8,128)(2,1)} %param.31), channel_id=1, source_target_pairs={{0,2},{2,4},{4,6},{6,8},{8,10},{10,12},{12,14},{14,16},{16,18},{18... | collective-permute-start | bytes 393224 | tf_op jit(solution)/shard_map/ppermute | solution.py:26
  101.5 52.7 %collective-permute-start.7 = (bf16[128,512]{1,0:T(8,128)(2,1)}, bf16[128,512]{1,0:T(8,128)(2,1)}, u32[]{:S(2)}, u32[]{:S(2)}) collective-permute-start(bf16[128,512]{1,0:T(8,128)(2,1)} %param.31), channel_id=1, source_target_pairs={{0,4},{2,6},{4,8},{6,10},{8,12},{10,14},{12,16},{14,18},{16,20},{1... | collective-permute-start | bytes 393224 | tf_op jit(solution)/shard_map/ppermute | solution.py:26
  104.1 5.6 %copy-start.9 = (bf16[128,1024]{1,0:T(8,128)(2,1)S(1)}, bf16[128,1024]{1,0:T(8,128)(2,1)}, u32[]{:S(2)}) copy-start(bf16[128,1024]{1,0:T(8,128)(2,1)} %param.25) | copy-start | bytes 786436
  108.3 6.0 %copy-start.7 = (bf16[128,4096]{1,0:T(8,128)(2,1)S(1)}, bf16[128,4096]{1,0:T(8,128)(2,1)}, u32[]{:S(2)}) copy-start(bf16[128,4096]{1,0:T(8,128)(2,1)} %param.23) | copy-start | bytes 3145732
  108.3 6.0 %copy-start.13 = (s32[32]{0:T(128)S(1)}, s32[32]{0:T(128)}, u32[]{:S(2)}) copy-start(s32[32]{0:T(128)} %copy-done.12) | copy-start | bytes 388
  117.5 1.4 copy-start.5
  148.7 22.8 %collective-permute-start.8 = (bf16[128,512]{1,0:T(8,128)(2,1)}, bf16[128,512]{1,0:T(8,128)(2,1)}, u32[]{:S(2)}, u32[]{:S(2)}) collective-permute-start(bf16[128,512]{1,0:T(8,128)(2,1)} %param.30), channel_id=1, source_target_pairs={{0,6},{2,8},{4,10},{6,12},{8,14},{10,16},{12,18},{14,20},{16,22},{... | collective-permute-start | bytes 393224 | tf_op jit(solution)/shard_map/ppermute | solution.py:26
  151.5 20.0 %collective-permute-start.9 = (bf16[128,512]{1,0:T(8,128)(2,1)}, bf16[128,512]{1,0:T(8,128)(2,1)}, u32[]{:S(2)}, u32[]{:S(2)}) collective-permute-start(bf16[128,512]{1,0:T(8,128)(2,1)} %param.31), channel_id=1, source_target_pairs={{0,6},{2,8},{4,10},{6,12},{8,14},{10,16},{12,18},{14,20},{16,22},{... | collective-permute-start | bytes 393224 | tf_op jit(solution)/shard_map/ppermute | solution.py:26
  152.8 26.7 %collective-permute-start.10 = (bf16[128,512]{1,0:T(8,128)(2,1)}, bf16[128,512]{1,0:T(8,128)(2,1)S(1)}, u32[]{:S(2)}, u32[]{:S(2)}) collective-permute-start(bf16[128,512]{1,0:T(8,128)(2,1)} %param.30), channel_id=1, source_target_pairs={{0,8},{2,10},{4,12},{6,14},{8,16},{10,18},{12,20},{14,22},{16,24},... | collective-permute-start | bytes 393224 | tf_op jit(solution)/shard_map/ppermute | solution.py:26
  154.1 25.4 %collective-permute-start.11 = (bf16[128,512]{1,0:T(8,128)(2,1)}, bf16[128,512]{1,0:T(8,128)(2,1)}, u32[]{:S(2)}, u32[]{:S(2)}) collective-permute-start(bf16[128,512]{1,0:T(8,128)(2,1)} %param.31), channel_id=1, source_target_pairs={{0,8},{2,10},{4,12},{6,14},{8,16},{10,18},{12,20},{14,22},{16,24},... | collective-permute-start | bytes 393224 | tf_op jit(solution)/shard_map/ppermute | solution.py:26
  157.1 1.4 copy-start.1
  165.1 1.4 copy-start.2
  173.1 1.4 copy-start.3
  180.3 1.4 copy-start.4
  187.5 5.0 %copy-start.10 = (bf16[128,4,256]{2,1,0:T(4,128)(2,1)S(1)}, bf16[128,4,256]{2,1,0:T(4,128)(2,1)}, u32[]{:S(2)}) copy-start(bf16[128,4,256]{2,1,0:T(4,128)(2,1)} %reshape.551) | copy-start | bytes 786436
  188.8 3.7 %copy-start.6 = (f32[128,4096]{0,1:T(8,128)S(1)}, f32[128,4096]{0,1:T(8,128)}, u32[]{:S(2)}) copy-start(f32[128,4096]{0,1:T(8,128)} %copy.247) | copy-start | bytes 6291460
  188.8 18.4 %all-to-all-start.1 = ((bf16[2,64,4096]{2,1,0:T(8,128)(2,1)}), bf16[2,64,4096]{2,1,0:T(8,128)(2,1)S(1)}, u32[]{:S(2)}, u32[]{:S(2)}) async-start(bf16[2,64,4096]{2,1,0:T(8,128)(2,1)} %convert_element_type.140), calls=%async_computation.1 | async-start | bytes 2097152 | tf_op jit(solution)/shard_map/all_to_all | solution.py:188
  201.3 2.9 %copy-start.11 = (f32[4096]{0:T(1024)S(1)}, f32[4096]{0:T(1024)}, u32[]{:S(2)}) copy-start(f32[4096]{0:T(1024)} %param.28) | copy-start | bytes 49156
  207.2 13.0 %all-to-all-start = ((bf16[2,64,4096]{2,1,0:T(8,128)(2,1)}), bf16[2,64,4096]{2,1,0:T(8,128)(2,1)S(1)}, u32[]{:S(2)}, u32[]{:S(2)}) async-start(bf16[2,64,4096]{2,1,0:T(8,128)(2,1)} %pad_maximum_fusion), calls=%async_computation | async-start | bytes 2097152 | tf_op jit(solution)/shard_map/all_to_all | solution.py:15
